TPU v7x, 32 devices: a whole 2x2x4 slice. The times are simulated.
32 devices in a mesh: dp: 8 (over z, y), tensor: 4 (over x, core).
Axes of the slice: x: 2, y: 2, z: 4, core: 2. Of those that a mesh axis runs over, the one named last changes fastest.
Arguments:
- tokens: bfloat16 [6144, 1120], P('dp', 'tensor'), may hold values from -6 to 6
- first_gain: float32 [1120], replicated, may hold values from 0.5 to 1.5
- first_shift: float32 [1120], replicated, may hold values from -3 to 3
- triple_weight: bfloat16 [1120, 3, 1120], P(None, None, 'tensor'), may hold values from -0.1875 to 0.1875
- triple_bias: float32 [2, 1120], P(None, 'tensor'), may hold values from -3 to 3
- output_weight: bfloat16 [1120, 1120], P('tensor'), may hold values from -0.5 to 0.5
- output_bias: float32 [1120], replicated, may hold values from -3 to 3
- second_gain: float32 [1120], replicated, may hold values from 0.5 to 1.5
- second_shift: float32 [1120], replicated, may hold values from -3 to 3
- up_weight: bfloat16 [1120, 4480], P(None, 'tensor'), may hold values from -0.1875 to 0.1875
- up_bias: float32 [4480], P('tensor'), may hold values from -3 to 3
- down_weight: bfloat16 [4480, 1120], P('tensor'), may hold values from -0.09375 to 0.09375
- down_bias: float32 [1120], replicated, may hold values from -3 to 3
- cotangent: bfloat16 [6144, 1120], P('dp', 'tensor'), may hold values from -6 to 6
- lengths: int32 [16], P('dp'), may hold values from 96 to 384
Outputs:
- layer_out: bfloat16 [6144, 1120], P('dp', 'tensor')
- input_grad: bfloat16 [6144, 1120], P('dp', 'tensor')
- first_gain_grad: float32 [1120], replicated
- first_shift_grad: float32 [1120], replicated
- triple_weight_grad: float32 [1120, 3, 1120], P(None, None, 'tensor')
- triple_bias_grad: float32 [2, 1120], P(None, 'tensor')
- output_weight_grad: float32 [1120, 1120], P('tensor')
- output_bias_grad: float32 [1120], replicated
- second_gain_grad: float32 [1120], replicated
- second_shift_grad: float32 [1120], replicated
- up_weight_grad: float32 [1120, 4480], P(None, 'tensor')
- up_bias_grad: float32 [4480], P('tensor')
- down_weight_grad: float32 [4480, 1120], P('tensor')
- down_bias_grad: float32 [1120], replicated
All inputs are finite; a program needn't handle non-finite values.
Results may differ from a plain program's by a relative error of at most 0.019.
Values may be sent and summed in bfloat16 or wider, within the bound.
No kernel may reach another device: no remote copies, remote signals or barrier semaphores. Data moves between devices by JAX's collectives and lax.ppermute only.
A program may use at most 128 MiB of HBM per device.

v0:
```python
import jax
import jax.numpy as jnp
from jax import lax
from jax.sharding import PartitionSpec as P

HEAD_DIM = 56
CELL_LEN = 384


epsilon = 1e-05


def layer_norm(field, gain, shift):
    center = field - jnp.mean(field, -1, keepdims=True)
    spread = jnp.mean(center * center, -1, keepdims=True)
    return center * lax.rsqrt(spread + epsilon) * gain + shift


def smooth_gate(field):
    return jax.nn.gelu(field, approximate=True)


def body(
    tokens,
    first_gain,
    first_shift,
    triple_weight,
    triple_bias,
    output_weight,
    output_bias,
    second_gain,
    second_shift,
    up_weight,
    up_bias,
    down_weight,
    down_bias,
    cotangent,
    lengths,
):
    row_count = tokens.shape[0]
    share_width = tokens.shape[1]
    width = triple_weight.shape[0]
    head_width = triple_weight.shape[2]
    local_heads = head_width // HEAD_DIM
    cell_count = row_count // CELL_LEN
    factor = HEAD_DIM ** (-0.5)
    offset = lax.axis_index("tensor") * share_width
    shape = (cell_count, CELL_LEN, local_heads, HEAD_DIM)
    whole_rows = lax.all_gather(tokens, "tensor", axis=1, tiled=True)
    floats = whole_rows.astype(jnp.float32)
    first_normed = layer_norm(floats, first_gain, first_shift).astype(jnp.bfloat16)
    triple_flat = triple_weight.reshape(width, 3 * head_width)
    projected = jnp.dot(first_normed, triple_flat, preferred_element_type=jnp.float32)
    projected = projected.reshape(row_count, 3, head_width)
    queries = (projected[:, 0] + triple_bias[0]).astype(jnp.bfloat16).reshape(shape)
    key_rows = projected[:, 1].astype(jnp.bfloat16).reshape(shape)
    value_rows = (projected[:, 2] + triple_bias[1]).astype(jnp.bfloat16).reshape(shape)
    places = jnp.arange(CELL_LEN)
    allowed = (places[None, None, :] <= places[None, :, None]) & (
        places[None, None, :] < lengths[:, None, None]
    )
    allowed = allowed[:, None]
    scores = (
        jnp.einsum("cqhd,ckhd->chqk", queries, key_rows, preferred_element_type=jnp.float32)
        * factor
    )
    masked = jnp.where(allowed, scores, -1e30)
    largest = jnp.max(masked, -1, keepdims=True)
    expo = jnp.exp(masked - largest)
    probs = expo / jnp.sum(expo, -1, keepdims=True)
    probs_low = probs.astype(jnp.bfloat16)
    context = jnp.einsum(
        "chqk,ckhd->cqhd", probs_low, value_rows, preferred_element_type=jnp.float32
    )
    context = context.reshape(row_count, head_width).astype(jnp.bfloat16)
    partial_value = jnp.dot(context, output_weight, preferred_element_type=jnp.float32)
    resid_full = (
        floats
        + lax.psum(partial_value.astype(jnp.bfloat16), "tensor").astype(jnp.float32)
        + output_bias
    )
    resid_share = lax.dynamic_slice_in_dim(resid_full, offset, share_width, 1)
    second_normed = layer_norm(resid_full, second_gain, second_shift).astype(jnp.bfloat16)
    hidden_pre = jnp.dot(second_normed, up_weight, preferred_element_type=jnp.float32) + up_bias
    hidden = smooth_gate(hidden_pre).astype(jnp.bfloat16)
    down_part = jnp.dot(hidden, down_weight, preferred_element_type=jnp.float32)
    down_total = lax.psum_scatter(
        down_part.astype(jnp.bfloat16), "tensor", scatter_dimension=1, tiled=True
    ).astype(jnp.float32)
    layer_out = (
        resid_share + down_total + lax.dynamic_slice_in_dim(down_bias, offset, share_width)
    ).astype(jnp.bfloat16)
    grad_rows = lax.all_gather(cotangent, "tensor", axis=1, tiled=True)
    grad_float = grad_rows.astype(jnp.float32)
    down_bias_grad = jnp.sum(grad_float, 0)
    down_grad = jnp.einsum("rf,rd->fd", hidden, grad_rows, preferred_element_type=jnp.float32)
    hidden_grad = jnp.einsum(
        "rd,fd->rf", grad_rows, down_weight, preferred_element_type=jnp.float32
    )
    gate_value, gate_back = jax.vjp(smooth_gate, hidden_pre)
    pre_grad = gate_back(hidden_grad)[0]
    up_bias_grad = jnp.sum(pre_grad, 0)
    pre_low = pre_grad.astype(jnp.bfloat16)
    up_grad = jnp.einsum("rd,rf->df", second_normed, pre_low, preferred_element_type=jnp.float32)
    normed_part = jnp.einsum("rf,df->rd", pre_low, up_weight, preferred_element_type=jnp.float32)
    normed_grad = lax.psum(normed_part.astype(jnp.bfloat16), "tensor").astype(jnp.float32)
    norm_value, second_back = jax.vjp(layer_norm, resid_full, second_gain, second_shift)
    resid_back, second_gain_grad, second_shift_grad = second_back(normed_grad)
    resid_grad = grad_float + resid_back
    output_bias_grad = jnp.sum(resid_grad, 0)
    resid_low = resid_grad.astype(jnp.bfloat16)
    output_grad = jnp.einsum("rh,rd->hd", context, resid_low, preferred_element_type=jnp.float32)
    context_grad = jnp.einsum(
        "rd,hd->rh", resid_low, output_weight, preferred_element_type=jnp.float32
    )
    context_grad = context_grad.astype(jnp.bfloat16).reshape(shape)
    prob_grad = jnp.einsum(
        "cqhd,ckhd->chqk", context_grad, value_rows, preferred_element_type=jnp.float32
    )
    value_grad = jnp.einsum(
        "chqk,cqhd->ckhd", probs_low, context_grad, preferred_element_type=jnp.float32
    )
    score_grad = probs * (prob_grad - jnp.sum(prob_grad * probs, -1, keepdims=True))
    score_low = (score_grad * factor).astype(jnp.bfloat16)
    query_grad = jnp.einsum(
        "chqk,ckhd->cqhd", score_low, key_rows, preferred_element_type=jnp.float32
    )
    key_grad = jnp.einsum("chqk,cqhd->ckhd", score_low, queries, preferred_element_type=jnp.float32)
    query_grad = query_grad.reshape(row_count, head_width)
    key_grad = key_grad.reshape(row_count, head_width)
    value_grad = value_grad.reshape(row_count, head_width)
    triple_bias_grad = jnp.stack([jnp.sum(query_grad, 0), jnp.sum(value_grad, 0)], 0)
    triple_low = jnp.stack([query_grad, key_grad, value_grad], 1).astype(jnp.bfloat16)
    triple_low = triple_low.reshape(row_count, 3 * head_width)
    triple_grad = jnp.einsum(
        "rd,rc->dc", first_normed, triple_low, preferred_element_type=jnp.float32
    )
    triple_grad = triple_grad.reshape(width, 3, head_width)
    first_part = jnp.einsum(
        "rc,dc->rd", triple_low, triple_flat, preferred_element_type=jnp.float32
    )
    first_grad = lax.psum(first_part.astype(jnp.bfloat16), "tensor").astype(jnp.float32)
    first_value, first_back = jax.vjp(layer_norm, floats, first_gain, first_shift)
    input_back, first_gain_grad, first_shift_grad = first_back(first_grad)
    input_full = resid_grad + input_back
    input_grad = lax.dynamic_slice_in_dim(input_full, offset, share_width, 1).astype(jnp.bfloat16)
    summed = lax.psum(
        (
            first_gain_grad,
            first_shift_grad,
            triple_grad,
            triple_bias_grad,
            output_grad,
            output_bias_grad,
            down_grad,
            down_bias_grad,
            up_grad,
            up_bias_grad,
            second_gain_grad,
            second_shift_grad,
        ),
        "dp",
    )
    return (
        layer_out,
        input_grad,
        summed[0],
        summed[1],
        summed[2],
        summed[3],
        summed[4],
        summed[5],
        summed[10],
        summed[11],
        summed[8],
        summed[9],
        summed[6],
        summed[7],
    )


def solution(mesh):
    placed = (
        P("dp", "tensor"),
        P(),
        P(),
        P(None, None, "tensor"),
        P(None, "tensor"),
        P("tensor", None),
        P(),
        P(),
        P(),
        P(None, "tensor"),
        P("tensor"),
        P("tensor", None),
        P(),
        P("dp", "tensor"),
        P("dp"),
    )
    return jax.shard_map(
        body,
        mesh=mesh,
        in_specs=placed,
        out_specs=(
            P("dp", "tensor"),
            P("dp", "tensor"),
            P(),
            P(),
            P(None, None, "tensor"),
            P(None, "tensor"),
            P("tensor", None),
            P(),
            P(),
            P(),
            P(None, "tensor"),
            P("tensor"),
            P("tensor", None),
            P(),
        ),
        check_vma=False,
    )
```

profile of v0, /device:TPU:0, one launch (start us, length us, event | category | flops | bytes accessed | tf_op | source)
XLA Modules:
  0.0 791.9 jit_solution(13180206961236640351)
XLA Ops:
  8.8 0.8 slice_reduce_fusion
  10.5 0.9 broadcast_and_fusion
  11.4 21.4 %all-gather.3.cloned.1.call-done = bf16[768,1120]{0,1:T(8,128)(2,1)} async-done(((bf16[768,280]{0,1:T(8,128)(2,1)}), bf16[768,1120]{0,1:T(8,128)(2,1)}) %all-gather.3.cloned.1.call-update) | async-done | bytes 1720336 | tf_op jit(solution)/shard_map/all_gather | solution.py:49
  32.8 1.9 convert_reduce_fusion.2
  34.7 2.0 fusion.29
  36.7 3.7 fusion.40
  40.4 0.8 slice.27
  41.2 1.3 fusion.106
  42.5 1.6 squeeze.7
  44.2 1.9 convert_element_type.93
  46.0 2.5 squeeze.8
  48.6 6.1 fusion.107
  54.7 3.4 fusion.61
  59.3 2.3 convolution_convert_fusion.2
  61.9 6.4 fusion.120
  68.3 39.0 %all-reduce.7.cloned.1.call-done = bf16[768,1120]{0,1:T(8,128)(2,1)} async-done(((bf16[768,1120]{0,1:T(8,128)(2,1)}), bf16[768,1120]{0,1:T(8,128)(2,1)}) %all-reduce.7.cloned.1.call-update) | async-done | bytes 1720336 | tf_op jit(solution)/shard_map/psum | solution.py:79
  107.2 2.6 fusion.104
  110.7 2.4 copy-done.25
  113.1 6.6 fusion.100
  119.7 1.3 copy-done.26
  120.9 3.6 convolution_convert_fusion
  125.0 45.1 %all-reduce.9.cloned.1.call-done = bf16[768,1120]{0,1:T(8,128)(2,1)} async-done(((bf16[768,1120]{0,1:T(8,128)(2,1)}), bf16[768,1120]{0,1:T(8,128)(2,1)}) %all-reduce.9.cloned.1.call-update) | async-done | bytes 1720336 | tf_op jit(solution)/shard_map/psum | solution.py:106
  170.1 3.6 convert_reduce_fusion.1
  173.8 3.8 fusion.32
  177.7 2.0 fusion.102
  179.7 1.7 copy-done.7
  182.2 4.0 fusion.112
  186.3 3.7 fusion.79
  190.0 9.7 %fusion.53 = bf16[2,384,5,56]{1,3,2,0:T(8,128)(2,1)S(1)} fusion(f32[2,5,384,384]{2,3,1,0:T(8,128)} %fusion.79, f32[2,5,384,384]{2,3,1,0:T(8,128)} %get-tuple-element.47, f32[2,5,384]{2,1,0:T(8,128)S(1)} %copy-done.29, f32[2,384,5,56]{1,0,3,2:T(2,128)S(1)} %copy-done.15, f32[5,56]{1,0:T(8,128)S(1)} %add.148), kind=kOutput, calls=%fused_computation.72 | convolution fusion | flops 175906944 | bytes 13103200 | tf_op jit(solution)/shard_map/chqk,cqhd->ckhd/dot_general | solution.py:128
  199.7 9.8 %fusion.113 = (f32[5,56]{1,0:T(8,128)S(1)}, bf16[2,384,5,56]{1,3,2,0:T(8,128)(2,1)S(1)}) fusion(f32[2,5,384,384]{2,3,1,0:T(8,128)} %fusion.79, f32[2,5,384,384]{2,3,1,0:T(8,128)} %get-tuple-element.47, f32[2,5,384]{2,1,0:T(8,128)S(1)} %copy-done.29, bf16[2,384,5,56]{1,0,3,2:T(2,128)(2,1)S(1)} %copy-done.18), kind=kOutput, calls=%fused_computation.132 | convolution fusion | flops 175906656 | bytes 12673120 | tf_op jit(solution)/shard_map/chqk,ckhd->cqhd/dot_general | solution.py:125
  211.5 4.8 fusion.34
  216.4 6.8 convolution_convert_fusion.1
  223.3 7.5 fusion.99
  230.8 5.0 fusion.70
  235.8 1.8 fusion.67
  237.7 3.9 fusion.56
  241.6 0.8 dynamic_slice.10
  242.6 19.3 %all-reduce.11.cloned.1.call-done = bf16[768,1120]{0,1:T(8,128)(2,1)} async-done(((bf16[768,1120]{0,1:T(8,128)(2,1)}), bf16[768,1120]{0,1:T(8,128)(2,1)}) %all-reduce.11.cloned.1.call-update) | async-done | bytes 1720336 | tf_op jit(solution)/shard_map/psum | solution.py:142
  261.9 2.9 fusion.33
  264.8 38.2 %all-reduce = (f32[1120]{0:T(1024)}, f32[1120]{0:T(1024)}, f32[2,280]{1,0:T(2,128)}, f32[1120]{0:T(1024)}, f32[1120]{0:T(1024)}, /*index=5*/f32[1120]{0:T(1024)}, f32[1120]{0:T(1024)}, f32[1120]{0:T(1024)}) all-reduce(f32[1120]{0:T(1024)S(1)} %get-tuple-element.16, ...), channel_id=1, replica_groups=mesh['dp'=8,'tensor'=4] {'dp'}, use_global_device_ids=true, to_apply=%region_16.17 | all-reduce | flops 8400 | bytes 67200 | tf_op jit(solution)/shard_map/psum | solution.py:147
  303.0 2.5 fusion.103
  305.6 2.1 fusion.64
  307.6 2.2 add_convert_fusion.1
  309.8 463.3 %all-reduce.13.cloned.1.call-done = (f32[1120,3,280]{0,2,1:T(8,128)}, f32[280,1120]{1,0:T(8,128)}, f32[1120,1120]{1,0:T(8,128)}, f32[1120,1120]{1,0:T(8,128)}) async-done(((f32[1120,3,280]{0,2,1:T(8,128)}, f32[280,1120]{1,0:T(8,128)}, f32[1120,1120]{1,0:T(8,128)}, f32[1120,1120]{1,0:T(8,128)}), (f32[1120,3,280]{0,2,1:T(8,128)}, f32[280,1120]{1,0:T(8,128)}, f32[1120,1120]{1,0:T(8,128)}, ...) | async-done | bytes 15052816 | tf_op jit(solution)/shard_map/psum | solution.py:147
  773.1 4.5 copy.99
  777.6 1.0 copy.100
  778.7 2.6 copy.101
  782.5 2.3 copy.102
  (109 shorter events, 9.6 us)
Async XLA Ops:
  7.2 103.1 %copy-start = (bf16[1120,1120]{1,0:T(8,128)(2,1)S(1)}, bf16[1120,1120]{1,0:T(8,128)(2,1)}, u32[]{:S(2)}) copy-start(bf16[1120,1120]{1,0:T(8,128)(2,1)} %param.24) | copy-start | bytes 7526404
  7.2 29.5 %copy-start.24 = (f32[1120]{0:T(1024)S(1)}, f32[1120]{0:T(1024)}, u32[]{:S(2)}) copy-start(f32[1120]{0:T(1024)} %param.17) | copy-start | bytes 13444
  7.2 29.5 %copy-start.20 = (f32[1120]{0:T(1024)S(1)}, f32[1120]{0:T(1024)}, u32[]{:S(2)}) copy-start(f32[1120]{0:T(1024)} %param.16) | copy-start | bytes 13444
  7.2 25.6 %all-gather.3.cloned.1.call-start = ((), (), s32[]{:S(2)}) async-start(), calls=%async_computation.1 | async-start | bytes 2150400 | tf_op jit(solution)/shard_map/all_gather | solution.py:49
  8.0 53.9 %all-gather.5.cloned.1.call-start = ((), (), s32[]{:S(2)}) async-start(), calls=%async_computation.4 | async-start | bytes 2150400 | tf_op jit(solution)/shard_map/all_gather | solution.py:93
  8.7 98.5 %all-reduce.7.cloned.1.call-start = ((), (), s32[]{:S(2)}) async-start(), calls=%async_computation.2 | async-start | bytes 3440640 | tf_op jit(solution)/shard_map/psum | solution.py:79
  32.8 3.9 copy-start.5
  54.7 3.4 copy-start.28
  54.7 4.6 copy-start.16
  58.5 0.8 copy-start.10
  61.6 45.6 %copy-start.21 = (f32[1120]{0:T(1024)S(1)}, f32[1120]{0:T(1024)}, u32[]{:S(2)}) copy-start(f32[1120]{0:T(1024)} %param.21) | copy-start | bytes 13444
  61.6 108.5 %all-reduce.9.cloned.1.call-start = ((), (), s32[]{:S(2)}) async-start(), calls=%async_computation.5 | async-start | bytes 3440640 | tf_op jit(solution)/shard_map/psum | solution.py:106
  109.8 9.9 %copy-start.2 = (f32[768,1120]{0,1:T(8,128)}, f32[768,1120]{0,1:T(8,128)S(1)}, u32[]{:S(2)}) copy-start(f32[768,1120]{0,1:T(8,128)S(1)} %get-tuple-element.42) | copy-start | bytes 10321924
  109.8 0.7 copy-start.19
  109.8 0.8 copy-start.22
  109.9 0.8 copy-start.23
  109.9 3.2 copy-start.25
  119.7 1.3 copy-start.26
  124.6 137.3 %all-reduce.11.cloned.1.call-start = ((), (), s32[]{:S(2)}) async-start(), calls=%async_computation.6 | async-start | bytes 3440640 | tf_op jit(solution)/shard_map/psum | solution.py:142
  170.1 3.7 copy-start.9
  173.8 3.9 copy-start.3
  173.8 3.9 copy-start.12
  177.7 3.7 copy-start.17
  179.7 1.7 copy-start.7
  179.7 2.6 copy-start.29
  186.3 3.7 copy-start.15
  190.0 9.7 %copy-start.18 = (bf16[2,384,5,56]{1,0,3,2:T(2,128)(2,1)S(1)}, bf16[2,384,5,56]{1,0,3,2:T(2,128)(2,1)}, u32[]{:S(2)}) copy-start(bf16[2,384,5,56]{1,0,3,2:T(2,128)(2,1)} %convert_element_type.93) | copy-start | bytes 1290244
  216.3 91.3 %reduce-scatter.2.cloned.1.call-start = ((), (), s32[]{:S(2)}) async-start(), calls=%async_computation.3 | async-start | bytes 2150400 | tf_op jit(solution)/shard_map/reduce_scatter | solution.py:87
  216.3 6.9 copy-start.13
  223.2 550.0 %all-reduce.13.cloned.1.call-start = ((), (), s32[]{:S(2)}) async-start(), calls=%async_computation.7 | async-start | bytes 30965760 | tf_op jit(solution)/shard_map/psum | solution.py:147
  223.2 7.5 copy-start.4
  223.3 7.5 copy-start.27
  230.8 5.1 copy-start.8
  230.8 5.1 copy-start.11
  235.8 1.8 copy-start.6
  773.1 5.5 slice-start.2
  773.1 4.5 copy-start.14
  773.1 5.5 slice-start.3
  777.6 4.3 slice-start
  778.7 3.9 slice-start.1
  778.7 6.2 copy-start.1
Sparse Core Ops, SparseCore 0:
  9.6 23.1 all-gather.2
  34.4 20.4 all-gather.4
  61.7 45.4 all-reduce.6
  124.7 45.4 all-reduce.8
  216.4 45.4 all-reduce.10
  264.3 28.8 reduce-scatter.1
  299.1 473.9 all-reduce.12
where the time goes:
time: 799 us; the launch traced here: 792 us
  waiting for transfers between devices  590 us (74%)
  matrix products  89.9 us (11%)
  blocking collectives  38.2 us (5%)
  local copies, waits for them, and re-layouts  30.8 us (4%)
  other arithmetic  27.7 us (3%)
  between operations  14.8 us (2%)
    psum x1, waiting for transfers between devices, body(): lax.psum((first_gain_grad, first_shift_grad, triple_grad, triple_bias_gra...  463 us
    psum x1, waiting for transfers between devices, body(): lax.psum(normed_part.astype(jnp.bfloat16), 'tensor').astype(jnp.float32)  45.1 us
    psum x1, waiting for transfers between devices, body(): lax.psum(partial_value.astype(jnp.bfloat16), 'tensor').astype(jnp.float32)  39 us
    psum x1, blocking collectives, body(): lax.psum((first_gain_grad, first_shift_grad, triple_grad, triple_bias_gra...  38.2 us
    all_gather x1, waiting for transfers between devices, body(): whole_rows = lax.all_gather(tokens, 'tensor', axis=1, tiled=True)  21.4 us
    psum x1, waiting for transfers between devices, body(): lax.psum(first_part.astype(jnp.bfloat16), 'tensor').astype(jnp.float32)  19.3 us
    unnamed x73, local copies, waits for them, and re-layouts  18.4 us
  transfers between devices with their start and end apart: 7, of which 5 were waited for; matrix products, arithmetic and copies ran while one was open for 9% of the time, Pallas kernels for 0%

commit v1 on v0

--- a/solution.py
+++ b/solution.py
@@ -1,3 +1,5 @@
+import functools
+
 import jax
 import jax.numpy as jnp
 from jax import lax
@@ -20,7 +22,128 @@
     return jax.nn.gelu(field, approximate=True)
 
 
+def swap_core(value, size):
+    return lax.ppermute(value, "tensor", [(place, place ^ 1) for place in range(size)])
+
+
+def swap_chip(value, size):
+    return lax.ppermute(value, "tensor", [(place, place ^ 2) for place in range(size)])
+
+
+def ordered(bit, mine, other, axis):
+    low = jnp.where(bit == 0, mine, other)
+    high = jnp.where(bit == 0, other, mine)
+    return jnp.concatenate([low, high], axis)
+
+
+def gather_features(share, size):
+    if size != 4:
+        return lax.all_gather(share, "tensor", axis=1, tiled=True)
+    place = lax.axis_index("tensor")
+    core, chip = place % 2, place // 2
+    far = swap_chip(share, size)
+    near_pair = ordered(core, share, swap_core(share, size), 1)
+    far_pair = ordered(core, far, swap_core(far, size), 1)
+    return ordered(chip, near_pair, far_pair, 1)
+
+
+def add_low(left, right):
+    return (left.astype(jnp.float32) + right.astype(jnp.float32)).astype(jnp.bfloat16)
+
+
+def take_half(value, index, axis):
+    half = value.shape[axis] // 2
+    return lax.dynamic_slice_in_dim(value, index * half, half, axis)
+
+
+def sum_features(part, size):
+    if size != 4:
+        return lax.psum(part, "tensor")
+    core = lax.axis_index("tensor") % 2
+    near = add_low(take_half(part, core, 0), swap_core(take_half(part, 1 - core, 0), size))
+    total = add_low(near, swap_chip(near, size))
+    return ordered(core, total, swap_core(total, size), 0)
+
+
+def scatter_features(part, size):
+    if size != 4:
+        return lax.psum_scatter(part, "tensor", scatter_dimension=1, tiled=True)
+    place = lax.axis_index("tensor")
+    core, chip = place % 2, place // 2
+    share = part.shape[1] // 4
+    blocks = [part[:, place * share : (place + 1) * share] for place in range(4)]
+
+    def pick(bit, first, second):
+        return jnp.where(bit == 0, first, second)
+
+    send = jnp.concatenate([pick(core, blocks[1], blocks[0]), pick(core, blocks[3], blocks[2])], 0)
+    got = swap_core(send, size)
+    rows = part.shape[0]
+    lower = add_low(pick(core, blocks[0], blocks[1]), got[:rows])
+    upper = add_low(pick(core, blocks[2], blocks[3]), got[rows:])
+    away = swap_chip(pick(chip, upper, lower), size)
+    return pick(chip, lower, upper).astype(jnp.float32) + away.astype(jnp.float32)
+
+
+def line_pairs(pairs):
+    return [(2 * source + side, 2 * target + side) for source, target in pairs for side in (0, 1)]
+
+
+INWARD = line_pairs([(0, 1), (3, 2)])
+MIDDLE = line_pairs([(1, 2), (2, 1)])
+OUTWARD = line_pairs([(1, 0), (2, 3)])
+ACROSS = [(place, place ^ 1) for place in range(8)]
+ACROSS_MIDDLE = [(2, 3), (3, 2), (4, 5), (5, 4)]
+
+
+def hop(value, pairs):
+    return lax.ppermute(value, "dp", pairs)
+
+
+def sum_across_first(value):
+    place = lax.axis_index("dp")
+    side, row = place % 2, place // 2
+    at_end = (row == 0) | (row == 3)
+    value = add_low(take_half(value, side, 0), hop(take_half(value, 1 - side, 0), ACROSS))
+    value = add_low(value, hop(value, INWARD))
+    value = add_low(value, hop(value, MIDDLE))
+    value = jnp.where(at_end, hop(value, OUTWARD), value)
+    return ordered(side, value, hop(value, ACROSS), 0)
+
+
+def sum_along_first(value):
+    place = lax.axis_index("dp")
+    row = place // 2
+    at_end = (row == 0) | (row == 3)
+    upper = row // 2
+    value = add_low(value, hop(value, INWARD))
+    value = add_low(take_half(value, upper, 0), hop(take_half(value, 1 - upper, 0), MIDDLE))
+    value = add_low(value, hop(value, ACROSS_MIDDLE))
+    value = ordered(upper, value, hop(value, MIDDLE), 0)
+    return jnp.where(at_end, hop(value, OUTWARD), value)
+
+
+def sum_cells(value, groups):
+    value = value.astype(jnp.bfloat16)
+    if groups != 8:
+        return lax.psum(value, "dp").astype(jnp.float32)
+    half = value.shape[0] // 2
+    first = sum_across_first(value[:half])
+    second = sum_along_first(value[half:])
+    return jnp.concatenate([first, second], 0).astype(jnp.float32)
+
+
+def sum_small(value, groups):
+    if groups != 8:
+        return lax.psum(value, "dp")
+    for step in (1, 4, 2):
+        value = value + hop(value, [(place, place ^ step) for place in range(8)])
+    return value
+
+
 def body(
+    groups,
+    size,
     tokens,
     first_gain,
     first_shift,
@@ -46,7 +169,8 @@
     factor = HEAD_DIM ** (-0.5)
     offset = lax.axis_index("tensor") * share_width
     shape = (cell_count, CELL_LEN, local_heads, HEAD_DIM)
-    whole_rows = lax.all_gather(tokens, "tensor", axis=1, tiled=True)
+    whole_rows = gather_features(tokens, size)
+    grad_rows = gather_features(cotangent, size)
     floats = whole_rows.astype(jnp.float32)
     first_normed = layer_norm(floats, first_gain, first_shift).astype(jnp.bfloat16)
     triple_flat = triple_weight.reshape(width, 3 * head_width)
@@ -76,7 +200,7 @@
     partial_value = jnp.dot(context, output_weight, preferred_element_type=jnp.float32)
     resid_full = (
         floats
-        + lax.psum(partial_value.astype(jnp.bfloat16), "tensor").astype(jnp.float32)
+        + sum_features(partial_value.astype(jnp.bfloat16), size).astype(jnp.float32)
         + output_bias
     )
     resid_share = lax.dynamic_slice_in_dim(resid_full, offset, share_width, 1)
@@ -84,13 +208,10 @@
     hidden_pre = jnp.dot(second_normed, up_weight, preferred_element_type=jnp.float32) + up_bias
     hidden = smooth_gate(hidden_pre).astype(jnp.bfloat16)
     down_part = jnp.dot(hidden, down_weight, preferred_element_type=jnp.float32)
-    down_total = lax.psum_scatter(
-        down_part.astype(jnp.bfloat16), "tensor", scatter_dimension=1, tiled=True
-    ).astype(jnp.float32)
+    down_total = scatter_features(down_part.astype(jnp.bfloat16), size)
     layer_out = (
         resid_share + down_total + lax.dynamic_slice_in_dim(down_bias, offset, share_width)
     ).astype(jnp.bfloat16)
-    grad_rows = lax.all_gather(cotangent, "tensor", axis=1, tiled=True)
     grad_float = grad_rows.astype(jnp.float32)
     down_bias_grad = jnp.sum(grad_float, 0)
     down_grad = jnp.einsum("rf,rd->fd", hidden, grad_rows, preferred_element_type=jnp.float32)
@@ -103,7 +224,7 @@
     pre_low = pre_grad.astype(jnp.bfloat16)
     up_grad = jnp.einsum("rd,rf->df", second_normed, pre_low, preferred_element_type=jnp.float32)
     normed_part = jnp.einsum("rf,df->rd", pre_low, up_weight, preferred_element_type=jnp.float32)
-    normed_grad = lax.psum(normed_part.astype(jnp.bfloat16), "tensor").astype(jnp.float32)
+    normed_grad = sum_features(normed_part.astype(jnp.bfloat16), size).astype(jnp.float32)
     norm_value, second_back = jax.vjp(layer_norm, resid_full, second_gain, second_shift)
     resid_back, second_gain_grad, second_shift_grad = second_back(normed_grad)
     resid_grad = grad_float + resid_back
@@ -139,43 +260,38 @@
     first_part = jnp.einsum(
         "rc,dc->rd", triple_low, triple_flat, preferred_element_type=jnp.float32
     )
-    first_grad = lax.psum(first_part.astype(jnp.bfloat16), "tensor").astype(jnp.float32)
+    first_grad = sum_features(first_part.astype(jnp.bfloat16), size).astype(jnp.float32)
     first_value, first_back = jax.vjp(layer_norm, floats, first_gain, first_shift)
     input_back, first_gain_grad, first_shift_grad = first_back(first_grad)
     input_full = resid_grad + input_back
     input_grad = lax.dynamic_slice_in_dim(input_full, offset, share_width, 1).astype(jnp.bfloat16)
-    summed = lax.psum(
-        (
-            first_gain_grad,
-            first_shift_grad,
-            triple_grad,
-            triple_bias_grad,
-            output_grad,
-            output_bias_grad,
-            down_grad,
-            down_bias_grad,
-            up_grad,
-            up_bias_grad,
-            second_gain_grad,
-            second_shift_grad,
-        ),
-        "dp",
-    )
+    down_grad = sum_cells(down_grad, groups)
+    up_grad = sum_cells(up_grad, groups)
+    output_grad = sum_cells(output_grad, groups)
+    triple_grad = sum_cells(triple_grad.reshape(width, 3 * head_width), groups)
+    triple_grad = triple_grad.reshape(width, 3, head_width)
+    middle = jnp.stack(
+        [down_bias_grad, up_bias_grad, second_gain_grad, second_shift_grad, output_bias_grad], 0
+    )
+    middle = sum_small(middle, groups)
+    final = jnp.stack([first_gain_grad, first_shift_grad], 0)
+    final = sum_small(final, groups)
+    triple_bias_grad = sum_small(triple_bias_grad, groups)
     return (
         layer_out,
         input_grad,
-        summed[0],
-        summed[1],
-        summed[2],
-        summed[3],
-        summed[4],
-        summed[5],
-        summed[10],
-        summed[11],
-        summed[8],
-        summed[9],
-        summed[6],
-        summed[7],
+        final[0],
+        final[1],
+        triple_grad,
+        triple_bias_grad,
+        output_grad,
+        middle[4],
+        middle[2],
+        middle[3],
+        up_grad,
+        middle[1],
+        down_grad,
+        middle[0],
     )
 
 
@@ -198,7 +314,7 @@
         P("dp"),
     )
     return jax.shard_map(
-        body,
+        functools.partial(body, mesh.shape["dp"], mesh.shape["tensor"]),
         mesh=mesh,
         in_specs=placed,
         out_specs=(

time: 799 us -> 546 us (0.68)
  waiting for transfers between devices: 590 us -> 251 us
  starting transfers between devices: 0.86 us -> 99.3 us
  blocking collectives: 38.2 us -> 0 us
  other arithmetic: 27.7 us -> 55.8 us
  local copies, waits for them, and re-layouts: 30.8 us -> 51.9 us
  matrix products: 89.9 us -> 74.8 us
  between operations: 14.8 us -> 2.48 us
    psum x4 -> x0, waiting for transfers between devices: 567 us -> none  [the longest x1 463 us: body(): lax.psum((first_gain_grad, first_shift_grad, triple_grad, triple_bias_gra...]
    ppermute x0 -> x66, waiting for transfers between devices: none -> 251 us  [the longest x49 213 us: hop(): return lax.ppermute(value, 'dp', pairs)]
    ppermute x0 -> x66, starting transfers between devices: none -> 99.3 us  [the longest x49 89 us: hop(): return lax.ppermute(value, 'dp', pairs)]
    psum x1 -> x0, blocking collectives: 38.2 us -> none  [body(): lax.psum((first_gain_grad, first_shift_grad, triple_grad, triple_bias_gra...]
    convert_element_type x0 -> x35, other arithmetic: none -> 23.1 us  [the longest x30 12.8 us: add_low(): (left.astype(jnp.float32) + right.astype(jnp.float32)).astype(jnp.bfloat16)]
    all_gather x2 -> x0, waiting for transfers between devices: 21.4 us -> none  [the longest x1 21.4 us: body(): whole_rows = lax.all_gather(tokens, 'tensor', axis=1, tiled=True)]
    select_n x0 -> x27, other arithmetic: none -> 16.6 us  [the longest x16 12.1 us: ordered(): low = jnp.where(bit == 0, mine, other)]
    unnamed x73 -> x75, local copies, waits for them, and re-layouts: 18.4 us -> 4.71 us
  transfers between devices with their start and end apart: 7 -> 66, of which waited for: 5 -> 26; matrix products, arithmetic and copies ran while one was open for 9% -> 23% of each run, Pallas kernels for 0% -> 0%
where the time goes in v1:
time: 546 us; the launch traced here: 535 us
  waiting for transfers between devices  251 us (46%)
  starting transfers between devices  99.3 us (18%)
  matrix products  74.8 us (14%)
  other arithmetic  55.8 us (10%)
  local copies, waits for them, and re-layouts  51.9 us (10%)
    ppermute x49, waiting for transfers between devices, hop(): return lax.ppermute(value, 'dp', pairs)  213 us
    ppermute x49, starting transfers between devices, hop(): return lax.ppermute(value, 'dp', pairs)  89 us
    ppermute x6, waiting for transfers between devices, swap_chip(): lax.ppermute(value, 'tensor', [(place, place ^ 2) for place in range(size)])  35.9 us
    convert_element_type x30, other arithmetic, add_low(): (left.astype(jnp.float32) + right.astype(jnp.float32)).astype(jnp.bfloat16)  12.8 us
    select_n x16, other arithmetic, ordered(): low = jnp.where(bit == 0, mine, other)  12.1 us
  transfers between devices with their start and end apart: 66, of which 26 were waited for; matrix products, arithmetic and copies ran while one was open for 23% of the time, Pallas kernels for 0%

profile of v1, /device:TPU:0, one launch (start us, length us, event | category | flops | bytes accessed | tf_op | source)
XLA Modules:
  0.0 535.4 jit_solution(540703814076872982)
XLA Ops:
  0.7 3.0 collective-permute-start.1
  5.4 8.4 %collective-permute-done.1 = bf16[768,280]{0,1:T(8,128)(2,1)S(1)} collective-permute-done((bf16[768,280]{0,1:T(8,128)(2,1)}, bf16[768,280]{0,1:T(8,128)(2,1)S(1)}, u32[]{:S(2)}, u32[]{:S(2)}) %collective-permute-start.1) | collective-permute-done | bytes 430112 | tf_op jit(solution)/shard_map/ppermute | solution.py:30
  22.3 2.5 squeeze.28
  29.2 6.1 %fusion.107 = (f32[2,5,384]{2,1,0:T(8,128)S(1)}, f32[2,5,384,384]{2,3,1,0:T(8,128)}) fusion(pred[2,384,384]{1,2,0:T(8,128)(4,1)} %broadcast_and_fusion, bf16[2,384,5,56]{1,0,3,2:T(2,128)(2,1)} %convert_element_type.409, f32[2,384,5,56]{1,0,3,2:T(2,128)} %squeeze.29, f32[5,56]{1,0:T(8,128)S(1)} %add.303), kind=kOutput, calls=%fused_computation.247 | convolution fusion | flops 171479424 | bytes 7499872 | tf_op jit(solution)/shard_map/sub | solution.py:193
  35.4 3.7 fusion.59
  49.4 20.0 %collective-permute-done.4 = bf16[384,1120]{0,1:T(8,128)(2,1)S(1)} collective-permute-done((bf16[384,1120]{0,1:T(8,128)(2,1)S(1)}, bf16[384,1120]{0,1:T(8,128)(2,1)S(1)}, u32[]{:S(2)}, u32[]{:S(2)}) %collective-permute-start.4) | collective-permute-done | bytes 860192 | tf_op jit(solution)/shard_map/ppermute | solution.py:30
  70.5 7.6 %collective-permute-done.9 = bf16[768,280]{0,1:T(8,128)(2,1)} collective-permute-done((bf16[768,280]{0,1:T(8,128)(2,1)}, bf16[768,280]{0,1:T(8,128)(2,1)}, u32[]{:S(2)}, u32[]{:S(2)}) %collective-permute-start.9) | collective-permute-done | bytes 430112 | tf_op jit(solution)/shard_map/ppermute | solution.py:30
  87.0 2.9 convolution_add_fusion
  90.0 2.8 convolution_convert_fusion.4
  92.7 5.7 %fusion.116 = (f32[1120]{0:T(1024)S(1)}, bf16[768,1120]{0,1:T(8,128)(2,1)S(1)}) fusion(f32[768,1120]{0,1:T(8,128)S(1)} %convolution_add_fusion, bf16[1120,1120]{1,0:T(8,128)(2,1)S(1)} %copy-done, bf16[768,560]{0,1:T(8,128)(2,1)S(1)} %get-tuple-element.52, bf16[768,560]{0,1:T(8,128)(2,1)S(1)} %get-tuple-element.51), kind=kOutput, calls=%fused_computation.250 | convolution fusion | flops 1948261248 | bytes 9394560 | tf_op jit(solution)/shard_map/rd,fd->rf/dot_general | solution.py:218
  98.5 3.1 convolution_convert_fusion
  102.2 2.7 convolution_convert_fusion.1
  110.2 3.8 collective-permute-start.51
  114.0 8.6 %collective-permute-done.46 = bf16[280,1120]{1,0:T(8,128)(2,1)S(1)} collective-permute-done((bf16[280,1120]{1,0:T(8,128)(2,1)S(1)}, bf16[280,1120]{1,0:T(8,128)(2,1)S(1)}, u32[]{:S(2)}, u32[]{:S(2)}) %collective-permute-start.46) | collective-permute-done | bytes 627232 | tf_op jit(solution)/shard_map/ppermute | solution.py:100
  122.6 3.8 collective-permute-start.61
  126.6 9.0 %collective-permute-done.56 = bf16[280,1120]{1,0:T(8,128)(2,1)S(1)} collective-permute-done((bf16[280,1120]{1,0:T(8,128)(2,1)S(1)}, bf16[280,1120]{1,0:T(8,128)(2,1)S(1)}, u32[]{:S(2)}, u32[]{:S(2)}) %collective-permute-start.56) | collective-permute-done | bytes 627232 | tf_op jit(solution)/shard_map/ppermute | solution.py:100
  135.6 3.7 collective-permute-start.47
  144.5 25.8 %collective-permute-done.61 = bf16[560,1120]{1,0:T(8,128)(2,1)S(1)} collective-permute-done((bf16[560,1120]{1,0:T(8,128)(2,1)S(1)}, bf16[560,1120]{1,0:T(8,128)(2,1)S(1)}, u32[]{:S(2)}, u32[]{:S(2)}) %collective-permute-start.61) | collective-permute-done | bytes 1254432 | tf_op jit(solution)/shard_map/ppermute | solution.py:100
  171.5 12.7 %collective-permute-done.47 = bf16[280,1120]{1,0:T(8,128)(2,1)S(1)} collective-permute-done((bf16[280,1120]{1,0:T(8,128)(2,1)S(1)}, bf16[280,1120]{1,0:T(8,128)(2,1)S(1)}, u32[]{:S(2)}, u32[]{:S(2)}) %collective-permute-start.47) | collective-permute-done | bytes 627232 | tf_op jit(solution)/shard_map/ppermute | solution.py:100
  185.0 12.5 %collective-permute-done.57 = bf16[280,1120]{1,0:T(8,128)(2,1)S(1)} collective-permute-done((bf16[280,1120]{1,0:T(8,128)(2,1)S(1)}, bf16[280,1120]{1,0:T(8,128)(2,1)S(1)}, u32[]{:S(2)}, u32[]{:S(2)}) %collective-permute-start.57) | collective-permute-done | bytes 627232 | tf_op jit(solution)/shard_map/ppermute | solution.py:100
  210.4 22.4 %collective-permute-done.49 = bf16[280,1120]{1,0:T(8,128)(2,1)S(1)} collective-permute-done((bf16[280,1120]{1,0:T(8,128)(2,1)S(1)}, bf16[280,1120]{1,0:T(8,128)(2,1)S(1)}, u32[]{:S(2)}, u32[]{:S(2)}) %collective-permute-start.49) | collective-permute-done | bytes 627232 | tf_op jit(solution)/shard_map/ppermute | solution.py:100
  233.7 12.9 %collective-permute-done.59 = bf16[280,1120]{1,0:T(8,128)(2,1)S(1)} collective-permute-done((bf16[280,1120]{1,0:T(8,128)(2,1)S(1)}, bf16[280,1120]{1,0:T(8,128)(2,1)S(1)}, u32[]{:S(2)}, u32[]{:S(2)}) %collective-permute-start.59) | collective-permute-done | bytes 627232 | tf_op jit(solution)/shard_map/ppermute | solution.py:100
  250.3 3.1 fusion.98
  256.8 4.9 fusion.112
  261.6 3.7 fusion.73
  265.3 10.7 %fusion.53 = bf16[2,384,5,56]{1,3,2,0:T(8,128)(2,1)} fusion(f32[2,5,384,384]{2,3,1,0:T(8,128)} %fusion.73, f32[2,5,384,384]{2,3,1,0:T(8,128)} %get-tuple-element.86, f32[2,5,384]{2,1,0:T(8,128)} %copy-done.36, f32[2,384,5,56]{1,0,3,2:T(2,128)} %squeeze.29, f32[5,56]{1,0:T(8,128)S(1)} %add.303), kind=kOutput, calls=%fused_computation.91 | convolution fusion | flops 175906944 | bytes 13103200 | tf_op jit(solution)/shard_map/chqk,cqhd->ckhd/dot_general | solution.py:249
  276.0 10.5 %fusion.113 = (f32[5,56]{1,0:T(8,128)S(1)}, bf16[2,384,5,56]{1,3,2,0:T(8,128)(2,1)}) fusion(f32[2,5,384,384]{2,3,1,0:T(8,128)} %fusion.73, f32[2,5,384,384]{2,3,1,0:T(8,128)} %get-tuple-element.86, f32[2,5,384]{2,1,0:T(8,128)} %copy-done.36, bf16[2,384,5,56]{1,0,3,2:T(2,128)(2,1)} %convert_element_type.409), kind=kOutput, calls=%fused_computation.249 | convolution fusion | flops 175906656 | bytes 12673120 | tf_op jit(solution)/shard_map/chqk,ckhd->cqhd/dot_general | solution.py:246
  298.9 5.2 fusion.34
  306.0 3.9 convolution_convert_fusion.2
  334.2 2.6 collective-permute-start.38
  337.9 5.2 collective-permute-done.38
  343.0 4.3 collective-permute-start.34
  353.6 14.2 %collective-permute-done.20 = bf16[280,840]{1,0:T(8,128)(2,1)S(1)} collective-permute-done((bf16[280,840]{1,0:T(8,128)(2,1)S(1)}, bf16[280,840]{1,0:T(8,128)(2,1)S(1)}, u32[]{:S(2)}, u32[]{:S(2)}) %collective-permute-start.20) | collective-permute-done | bytes 470432 | tf_op jit(solution)/shard_map/ppermute | solution.py:100
  368.0 10.8 %collective-permute-start.25 = (bf16[560,840]{1,0:T(8,128)(2,1)S(1)}, bf16[560,840]{1,0:T(8,128)(2,1)S(1)}, u32[]{:S(2)}, u32[]{:S(2)}) collective-permute-start(bf16[560,840]{1,0:T(8,128)(2,1)S(1)} %copy-done.24), channel_id=1, source_target_pairs={{0,8},{4,12},{24,16},{28,20},{1,9},{5,13},{25,17},{29,21},{2,10},{... | collective-permute-start | bytes 2822408 | tf_op jit(solution)/shard_map/ppermute | solution.py:100
  382.6 4.2 collective-permute-start.21
  389.9 6.0 %collective-permute-done.36 = bf16[70,1120]{1,0:T(8,128)(2,1)S(1)} collective-permute-done((bf16[70,1120]{1,0:T(8,128)(2,1)S(1)}, bf16[70,1120]{1,0:T(8,128)(2,1)S(1)}, u32[]{:S(2)}, u32[]{:S(2)}) %collective-permute-start.36) | collective-permute-done | bytes 156832 | tf_op jit(solution)/shard_map/ppermute | solution.py:100
  397.3 4.7 collective-permute-done.37
  404.9 6.6 %collective-permute-done.21 = bf16[280,840]{1,0:T(8,128)(2,1)S(1)} collective-permute-done((bf16[280,840]{1,0:T(8,128)(2,1)S(1)}, bf16[280,840]{1,0:T(8,128)(2,1)S(1)}, u32[]{:S(2)}, u32[]{:S(2)}) %collective-permute-start.21) | collective-permute-done | bytes 470432 | tf_op jit(solution)/shard_map/ppermute | solution.py:100
  414.2 43.1 %collective-permute-done.42 = bf16[140,1120]{1,0:T(8,128)(2,1)S(1)} collective-permute-done((bf16[140,1120]{1,0:T(8,128)(2,1)S(1)}, bf16[140,1120]{1,0:T(8,128)(2,1)S(1)}, u32[]{:S(2)}, u32[]{:S(2)}) %collective-permute-start.42) | collective-permute-done | bytes 313632 | tf_op jit(solution)/shard_map/ppermute | solution.py:100
  463.0 2.7 maximum_convert_fusion.1
  466.1 7.7 %collective-permute-done.23 = bf16[280,840]{1,0:T(8,128)(2,1)S(1)} collective-permute-done((bf16[280,840]{1,0:T(8,128)(2,1)S(1)}, bf16[280,840]{1,0:T(8,128)(2,1)S(1)}, u32[]{:S(2)}, u32[]{:S(2)}) %collective-permute-start.23) | collective-permute-done | bytes 470432 | tf_op jit(solution)/shard_map/ppermute | solution.py:100
  476.8 2.7 maximum_convert_fusion.2
  479.4 6.0 %collective-permute-done.24 = bf16[280,840]{1,0:T(8,128)(2,1)S(1)} collective-permute-done((bf16[280,840]{1,0:T(8,128)(2,1)S(1)}, bf16[280,840]{1,0:T(8,128)(2,1)S(1)}, u32[]{:S(2)}, u32[]{:S(2)}) %collective-permute-start.24) | collective-permute-done | bytes 470432 | tf_op jit(solution)/shard_map/ppermute | solution.py:100
  500.8 10.3 %collective-permute-start.18 = (f32[2,1120]{1,0:T(2,128)S(1)}, f32[2,1120]{1,0:T(2,128)S(1)}, u32[]{:S(2)}, u32[]{:S(2)}) collective-permute-start(f32[2,1120]{1,0:T(2,128)S(1)} %fusion.94), channel_id=1, source_target_pairs={{0,16},{4,20},{8,24},{12,28},{16,0},{20,4},{24,8},{28,12},{1,17},{... | collective-permute-start | bytes 26888 | tf_op jit(solution)/shard_map/ppermute | solution.py:100
  512.9 2.7 collective-permute-start.19
  516.5 7.2 %collective-permute-done.19 = f32[2,1120]{1,0:T(2,128)S(1)} collective-permute-done((f32[2,1120]{1,0:T(2,128)S(1)}, f32[2,1120]{1,0:T(2,128)S(1)}, u32[]{:S(2)}, u32[]{:S(2)}) %collective-permute-start.19) | collective-permute-done | bytes 8992 | tf_op jit(solution)/shard_map/ppermute | solution.py:100
  526.3 5.0 concatenate.75
  531.3 3.7 convert_element_type.477
  (325 shorter events, 157.6 us)
Async XLA Ops:
  0.7 13.1 %collective-permute-start.1 = (bf16[768,280]{0,1:T(8,128)(2,1)}, bf16[768,280]{0,1:T(8,128)(2,1)S(1)}, u32[]{:S(2)}, u32[]{:S(2)}) collective-permute-start(bf16[768,280]{0,1:T(8,128)(2,1)} %param.15), channel_id=1, source_target_pairs={{0,2},{1,3},{2,0},{3,1},{4,6},{5,7},{6,4},{7,5},{8,10},{9,11},{10,... | collective-permute-start | bytes 1290248 | tf_op jit(solution)/shard_map/ppermute | solution.py:30
  3.7 11.0 %collective-permute-start = (bf16[768,280]{0,1:T(8,128)(2,1)}, bf16[768,280]{0,1:T(8,128)(2,1)S(1)}, u32[]{:S(2)}, u32[]{:S(2)}) collective-permute-start(bf16[768,280]{0,1:T(8,128)(2,1)} %param.15), channel_id=1, source_target_pairs={{0,1},{1,0},{2,3},{3,2},{4,5},{5,4},{6,7},{7,6},{8,9},{9,8},{10,11... | collective-permute-start | bytes 1290248 | tf_op jit(solution)/shard_map/ppermute | solution.py:26
  47.3 22.1 %collective-permute-start.4 = (bf16[384,1120]{0,1:T(8,128)(2,1)S(1)}, bf16[384,1120]{0,1:T(8,128)(2,1)S(1)}, u32[]{:S(2)}, u32[]{:S(2)}) collective-permute-start(bf16[384,1120]{0,1:T(8,128)(2,1)S(1)} %add_convert_fusion.9), channel_id=1, source_target_pairs={{0,2},{1,3},{2,0},{3,1},{4,6},{5,7},{6,4},{7,5},{8,10},{9,11},{10,... | collective-permute-start | bytes 2580488 | tf_op jit(solution)/shard_map/ppermute | solution.py:30
  49.1 29.0 %collective-permute-start.9 = (bf16[768,280]{0,1:T(8,128)(2,1)}, bf16[768,280]{0,1:T(8,128)(2,1)}, u32[]{:S(2)}, u32[]{:S(2)}) collective-permute-start(bf16[768,280]{0,1:T(8,128)(2,1)} %param.28), channel_id=1, source_target_pairs={{0,2},{1,3},{2,0},{3,1},{4,6},{5,7},{6,4},{7,5},{8,10},{9,11},{10,... | collective-permute-start | bytes 1290248 | tf_op jit(solution)/shard_map/ppermute | solution.py:30
  49.4 29.5 %collective-permute-start.8 = (bf16[768,280]{0,1:T(8,128)(2,1)}, bf16[768,280]{0,1:T(8,128)(2,1)}, u32[]{:S(2)}, u32[]{:S(2)}) collective-permute-start(bf16[768,280]{0,1:T(8,128)(2,1)} %param.28), channel_id=1, source_target_pairs={{0,1},{1,0},{2,3},{3,2},{4,5},{5,4},{6,7},{7,6},{8,9},{9,8},{10,11... | collective-permute-start | bytes 1290248 | tf_op jit(solution)/shard_map/ppermute | solution.py:26
  70.5 11.3 %collective-permute-start.5 = (bf16[384,1120]{0,1:T(8,128)(2,1)}, bf16[384,1120]{0,1:T(8,128)(2,1)}, u32[]{:S(2)}, u32[]{:S(2)}) collective-permute-start(bf16[384,1120]{0,1:T(8,128)(2,1)} %add_convert_fusion.8), channel_id=1, source_target_pairs={{0,1},{1,0},{2,3},{3,2},{4,5},{5,4},{6,7},{7,6},{8,9},{9,8},{10,11... | collective-permute-start | bytes 2580488 | tf_op jit(solution)/shard_map/ppermute | solution.py:26
  101.7 37.8 %collective-permute-start.6 = (bf16[1536,280]{0,1:T(8,128)(2,1)S(1)}, bf16[1536,280]{0,1:T(8,128)(2,1)S(1)}, u32[]{:S(2)}, u32[]{:S(2)}) collective-permute-start(bf16[1536,280]{0,1:T(8,128)(2,1)S(1)} %pad_maximum_fusion.9), channel_id=1, source_target_pairs={{0,1},{1,0},{2,3},{3,2},{4,5},{5,4},{6,7},{7,6},{8,9},{9,8},{10,11... | collective-permute-start | bytes 2580488 | tf_op jit(solution)/shard_map/ppermute | solution.py:26
  105.2 17.5 %collective-permute-start.46 = (bf16[280,1120]{1,0:T(8,128)(2,1)S(1)}, bf16[280,1120]{1,0:T(8,128)(2,1)S(1)}, u32[]{:S(2)}, u32[]{:S(2)}) collective-permute-start(bf16[280,1120]{1,0:T(8,128)(2,1)S(1)} %constant_dynamic-slice_fusion.3), channel_id=1, source_target_pairs={{0,4},{4,0},{8,12},{12,8},{16,20},{20,16},{24,28},{28,24},{1,5},{5... | collective-permute-start | bytes 1881608 | tf_op jit(solution)/shard_map/ppermute | solution.py:100
  107.3 28.4 %collective-permute-start.56 = (bf16[280,1120]{1,0:T(8,128)(2,1)S(1)}, bf16[280,1120]{1,0:T(8,128)(2,1)S(1)}, u32[]{:S(2)}, u32[]{:S(2)}) collective-permute-start(bf16[280,1120]{1,0:T(8,128)(2,1)S(1)} %constant_dynamic-slice_fusion.1), channel_id=1, source_target_pairs={{0,4},{4,0},{8,12},{12,8},{16,20},{20,16},{24,28},{28,24},{1,5},{5... | collective-permute-start | bytes 1881608 | tf_op jit(solution)/shard_map/ppermute | solution.py:100
  110.1 31.2 %collective-permute-start.11 = (bf16[384,1120]{0,1:T(8,128)(2,1)S(1)}, bf16[384,1120]{0,1:T(8,128)(2,1)S(1)}, u32[]{:S(2)}, u32[]{:S(2)}) collective-permute-start(bf16[384,1120]{0,1:T(8,128)(2,1)S(1)} %constant_dynamic-slice_fusion.9), channel_id=1, source_target_pairs={{0,1},{1,0},{2,3},{3,2},{4,5},{5,4},{6,7},{7,6},{8,9},{9,8},{10,11... | collective-permute-start | bytes 2580488 | tf_op jit(solution)/shard_map/ppermute | solution.py:26
  110.2 32.9 %collective-permute-start.51 = (bf16[560,1120]{1,0:T(8,128)(2,1)S(1)}, bf16[560,1120]{1,0:T(8,128)(2,1)S(1)}, u32[]{:S(2)}, u32[]{:S(2)}) collective-permute-start(bf16[560,1120]{1,0:T(8,128)(2,1)S(1)} %get-tuple-element.41), channel_id=1, source_target_pairs={{0,8},{4,12},{24,16},{28,20},{1,9},{5,13},{25,17},{29,21},{2,10},{... | collective-permute-start | bytes 3763208 | tf_op jit(solution)/shard_map/ppermute | solution.py:100
  122.6 47.7 %collective-permute-start.61 = (bf16[560,1120]{1,0:T(8,128)(2,1)S(1)}, bf16[560,1120]{1,0:T(8,128)(2,1)S(1)}, u32[]{:S(2)}, u32[]{:S(2)}) collective-permute-start(bf16[560,1120]{1,0:T(8,128)(2,1)S(1)} %get-tuple-element.39), channel_id=1, source_target_pairs={{0,8},{4,12},{24,16},{28,20},{1,9},{5,13},{25,17},{29,21},{2,10},{... | collective-permute-start | bytes 3763208 | tf_op jit(solution)/shard_map/ppermute | solution.py:100
  135.6 48.5 %collective-permute-start.47 = (bf16[280,1120]{1,0:T(8,128)(2,1)S(1)}, bf16[280,1120]{1,0:T(8,128)(2,1)S(1)}, u32[]{:S(2)}, u32[]{:S(2)}) collective-permute-start(bf16[280,1120]{1,0:T(8,128)(2,1)S(1)} %add_convert_fusion.19), channel_id=1, source_target_pairs={{0,8},{4,12},{24,16},{28,20},{1,9},{5,13},{25,17},{29,21},{2,10},{... | collective-permute-start | bytes 1881608 | tf_op jit(solution)/shard_map/ppermute | solution.py:100
  139.6 57.9 %collective-permute-start.57 = (bf16[280,1120]{1,0:T(8,128)(2,1)S(1)}, bf16[280,1120]{1,0:T(8,128)(2,1)S(1)}, u32[]{:S(2)}, u32[]{:S(2)}) collective-permute-start(bf16[280,1120]{1,0:T(8,128)(2,1)S(1)} %add_convert_fusion.14), channel_id=1, source_target_pairs={{0,8},{4,12},{24,16},{28,20},{1,9},{5,13},{25,17},{29,21},{2,10},{... | collective-permute-start | bytes 1881608 | tf_op jit(solution)/shard_map/ppermute | solution.py:100
  141.3 57.0 %collective-permute-start.7 = (bf16[768,280]{0,1:T(8,128)(2,1)S(1)}, bf16[768,280]{0,1:T(8,128)(2,1)S(1)}, u32[]{:S(2)}, u32[]{:S(2)}) collective-permute-start(bf16[768,280]{0,1:T(8,128)(2,1)S(1)} %get-tuple-element.33), channel_id=1, source_target_pairs={{0,2},{1,3},{2,0},{3,1},{4,6},{5,7},{6,4},{7,5},{8,10},{9,11},{10,... | collective-permute-start | bytes 1290248 | tf_op jit(solution)/shard_map/ppermute | solution.py:30
  143.1 57.1 %collective-permute-start.12 = (bf16[384,1120]{0,1:T(8,128)(2,1)S(1)}, bf16[384,1120]{0,1:T(8,128)(2,1)S(1)}, u32[]{:S(2)}, u32[]{:S(2)}) collective-permute-start(bf16[384,1120]{0,1:T(8,128)(2,1)S(1)} %add_convert_fusion.7), channel_id=1, source_target_pairs={{0,2},{1,3},{2,0},{3,1},{4,6},{5,7},{6,4},{7,5},{8,10},{9,11},{10,... | collective-permute-start | bytes 2580488 | tf_op jit(solution)/shard_map/ppermute | solution.py:30
  170.3 30.3 %collective-permute-start.52 = (bf16[280,1120]{1,0:T(8,128)(2,1)S(1)}, bf16[280,1120]{1,0:T(8,128)(2,1)S(1)}, u32[]{:S(2)}, u32[]{:S(2)}) collective-permute-start(bf16[280,1120]{1,0:T(8,128)(2,1)S(1)} %constant_dynamic-slice_fusion.2), channel_id=1, source_target_pairs={{8,16},{12,20},{16,8},{20,12},{9,17},{13,21},{17,9},{21,13},{10,18... | collective-permute-start | bytes 1881608 | tf_op jit(solution)/shard_map/ppermute | solution.py:100
  184.1 17.3 %collective-permute-start.62 = (bf16[280,1120]{1,0:T(8,128)(2,1)S(1)}, bf16[280,1120]{1,0:T(8,128)(2,1)S(1)}, u32[]{:S(2)}, u32[]{:S(2)}) collective-permute-start(bf16[280,1120]{1,0:T(8,128)(2,1)S(1)} %constant_dynamic-slice_fusion), channel_id=1, source_target_pairs={{8,16},{12,20},{16,8},{20,12},{9,17},{13,21},{17,9},{21,13},{10,18... | collective-permute-start | bytes 1881608 | tf_op jit(solution)/shard_map/ppermute | solution.py:100
  200.5 47.0 %collective-permute-start.13 = (bf16[384,1120]{0,1:T(8,128)(2,1)S(1)}, bf16[384,1120]{0,1:T(8,128)(2,1)S(1)}, u32[]{:S(2)}, u32[]{:S(2)}) collective-permute-start(bf16[384,1120]{0,1:T(8,128)(2,1)S(1)} %add_convert_fusion.6), channel_id=1, source_target_pairs={{0,1},{1,0},{2,3},{3,2},{4,5},{5,4},{6,7},{7,6},{8,9},{9,8},{10,11... | collective-permute-start | bytes 2580488 | tf_op jit(solution)/shard_map/ppermute | solution.py:26
  202.5 30.2 %collective-permute-start.49 = (bf16[280,1120]{1,0:T(8,128)(2,1)S(1)}, bf16[280,1120]{1,0:T(8,128)(2,1)S(1)}, u32[]{:S(2)}, u32[]{:S(2)}) collective-permute-start(bf16[280,1120]{1,0:T(8,128)(2,1)S(1)} %add_convert_fusion.17), channel_id=1, source_target_pairs={{8,0},{12,4},{16,24},{20,28},{9,1},{13,5},{17,25},{21,29},{10,2},{... | collective-permute-start | bytes 1881608 | tf_op jit(solution)/shard_map/ppermute | solution.py:100
  204.0 42.5 %collective-permute-start.59 = (bf16[280,1120]{1,0:T(8,128)(2,1)S(1)}, bf16[280,1120]{1,0:T(8,128)(2,1)S(1)}, u32[]{:S(2)}, u32[]{:S(2)}) collective-permute-start(bf16[280,1120]{1,0:T(8,128)(2,1)S(1)} %add_convert_fusion.12), channel_id=1, source_target_pairs={{8,0},{12,4},{16,24},{20,28},{9,1},{13,5},{17,25},{21,29},{10,2},{... | collective-permute-start | bytes 1881608 | tf_op jit(solution)/shard_map/ppermute | solution.py:100
  206.3 161.6 %collective-permute-start.54 = (bf16[280,1120]{1,0:T(8,128)(2,1)}, bf16[280,1120]{1,0:T(8,128)(2,1)}, u32[]{:S(2)}, u32[]{:S(2)}) collective-permute-start(bf16[280,1120]{1,0:T(8,128)(2,1)} %add_convert_fusion.15), channel_id=1, source_target_pairs={{8,16},{12,20},{16,8},{20,12},{9,17},{13,21},{17,9},{21,13},{10,18... | collective-permute-start | bytes 1881608 | tf_op jit(solution)/shard_map/ppermute | solution.py:100
  208.9 171.3 %collective-permute-start.64 = (bf16[280,1120]{1,0:T(8,128)(2,1)}, bf16[280,1120]{1,0:T(8,128)(2,1)}, u32[]{:S(2)}, u32[]{:S(2)}) collective-permute-start(bf16[280,1120]{1,0:T(8,128)(2,1)} %add_convert_fusion.10), channel_id=1, source_target_pairs={{8,16},{12,20},{16,8},{20,12},{9,17},{13,21},{17,9},{21,13},{10,18... | collective-permute-start | bytes 1881608 | tf_op jit(solution)/shard_map/ppermute | solution.py:100
  312.8 6.4 %collective-permute-start.30 = (f32[2,280]{1,0:T(2,128)S(1)}, f32[2,280]{1,0:T(2,128)S(1)}, u32[]{:S(2)}, u32[]{:S(2)}) collective-permute-start(f32[2,280]{1,0:T(2,128)S(1)} %pad_maximum_fusion.14), channel_id=1, source_target_pairs={{0,4},{4,0},{8,12},{12,8},{16,20},{20,16},{24,28},{28,24},{1,5},{5... | collective-permute-start | bytes 6728 | tf_op jit(solution)/shard_map/ppermute | solution.py:100
  320.8 13.4 %collective-permute-start.33 = (bf16[70,1120]{1,0:T(8,128)(2,1)S(1)}, bf16[70,1120]{1,0:T(8,128)(2,1)S(1)}, u32[]{:S(2)}, u32[]{:S(2)}) collective-permute-start(bf16[70,1120]{1,0:T(8,128)(2,1)S(1)} %constant_dynamic-slice_fusion.5), channel_id=1, source_target_pairs={{0,4},{4,0},{8,12},{12,8},{16,20},{20,16},{24,28},{28,24},{1,5},{5... | collective-permute-start | bytes 470408 | tf_op jit(solution)/shard_map/ppermute | solution.py:100
  330.9 51.7 %collective-permute-start.50 = (bf16[280,1120]{1,0:T(8,128)(2,1)}, bf16[280,1120]{1,0:T(8,128)(2,1)S(1)}, u32[]{:S(2)}, u32[]{:S(2)}) collective-permute-start(bf16[280,1120]{1,0:T(8,128)(2,1)} %broadcast_select_fusion.18), channel_id=1, source_target_pairs={{0,4},{4,0},{8,12},{12,8},{16,20},{20,16},{24,28},{28,24},{1,5},{5... | collective-permute-start | bytes 1881608 | tf_op jit(solution)/shard_map/ppermute | solution.py:100
  332.1 54.8 %collective-permute-start.60 = (bf16[280,1120]{1,0:T(8,128)(2,1)}, bf16[280,1120]{1,0:T(8,128)(2,1)S(1)}, u32[]{:S(2)}, u32[]{:S(2)}) collective-permute-start(bf16[280,1120]{1,0:T(8,128)(2,1)} %broadcast_select_fusion.17), channel_id=1, source_target_pairs={{0,4},{4,0},{8,12},{12,8},{16,20},{20,16},{24,28},{28,24},{1,5},{5... | collective-permute-start | bytes 1881608 | tf_op jit(solution)/shard_map/ppermute | solution.py:100
  334.2 8.8 %collective-permute-start.38 = (bf16[140,1120]{1,0:T(8,128)(2,1)}, bf16[140,1120]{1,0:T(8,128)(2,1)S(1)}, u32[]{:S(2)}, u32[]{:S(2)}) collective-permute-start(bf16[140,1120]{1,0:T(8,128)(2,1)} %get-tuple-element.80), channel_id=1, source_target_pairs={{0,8},{4,12},{24,16},{28,20},{1,9},{5,13},{25,17},{29,21},{2,10},{... | collective-permute-start | bytes 940808 | tf_op jit(solution)/shard_map/ppermute | solution.py:100
  343.0 7.1 %collective-permute-start.34 = (bf16[70,1120]{1,0:T(8,128)(2,1)S(1)}, bf16[70,1120]{1,0:T(8,128)(2,1)S(1)}, u32[]{:S(2)}, u32[]{:S(2)}) collective-permute-start(bf16[70,1120]{1,0:T(8,128)(2,1)S(1)} %add_convert_fusion.33), channel_id=1, source_target_pairs={{0,8},{4,12},{24,16},{28,20},{1,9},{5,13},{25,17},{29,21},{2,10},{... | collective-permute-start | bytes 470408 | tf_op jit(solution)/shard_map/ppermute | solution.py:100
  351.7 16.2 %collective-permute-start.20 = (bf16[280,840]{1,0:T(8,128)(2,1)S(1)}, bf16[280,840]{1,0:T(8,128)(2,1)S(1)}, u32[]{:S(2)}, u32[]{:S(2)}) collective-permute-start(bf16[280,840]{1,0:T(8,128)(2,1)S(1)} %constant_dynamic-slice_fusion.7), channel_id=1, source_target_pairs={{0,4},{4,0},{8,12},{12,8},{16,20},{20,16},{24,28},{28,24},{1,5},{5... | collective-permute-start | bytes 1411208 | tf_op jit(solution)/shard_map/ppermute | solution.py:100
  367.8 35.5 %collective-permute-start.14 = (bf16[384,1120]{0,1:T(8,128)(2,1)S(1)}, bf16[384,1120]{0,1:T(8,128)(2,1)S(1)}, u32[]{:S(2)}, u32[]{:S(2)}) collective-permute-start(bf16[384,1120]{0,1:T(8,128)(2,1)S(1)} %copy-done.25), channel_id=1, source_target_pairs={{0,1},{1,0},{2,3},{3,2},{4,5},{5,4},{6,7},{7,6},{8,9},{9,8},{10,11... | collective-permute-start | bytes 2580488 | tf_op jit(solution)/shard_map/ppermute | solution.py:26
  368.0 45.2 %collective-permute-start.25 = (bf16[560,840]{1,0:T(8,128)(2,1)S(1)}, bf16[560,840]{1,0:T(8,128)(2,1)S(1)}, u32[]{:S(2)}, u32[]{:S(2)}) collective-permute-start(bf16[560,840]{1,0:T(8,128)(2,1)S(1)} %copy-done.24), channel_id=1, source_target_pairs={{0,8},{4,12},{24,16},{28,20},{1,9},{5,13},{25,17},{29,21},{2,10},{... | collective-permute-start | bytes 2822408 | tf_op jit(solution)/shard_map/ppermute | solution.py:100
  380.2 8.2 %collective-permute-start.40 = (bf16[70,1120]{1,0:T(8,128)(2,1)S(1)}, bf16[70,1120]{1,0:T(8,128)(2,1)S(1)}, u32[]{:S(2)}, u32[]{:S(2)}) collective-permute-start(bf16[70,1120]{1,0:T(8,128)(2,1)S(1)} %add_convert_fusion.30), channel_id=1, source_target_pairs={{8,12},{12,8},{16,20},{20,16},{9,13},{13,9},{17,21},{21,17},{10,14... | collective-permute-start | bytes 470408 | tf_op jit(solution)/shard_map/ppermute | solution.py:100
  382.6 28.9 %collective-permute-start.21 = (bf16[280,840]{1,0:T(8,128)(2,1)S(1)}, bf16[280,840]{1,0:T(8,128)(2,1)S(1)}, u32[]{:S(2)}, u32[]{:S(2)}) collective-permute-start(bf16[280,840]{1,0:T(8,128)(2,1)S(1)} %add_convert_fusion.24), channel_id=1, source_target_pairs={{0,8},{4,12},{24,16},{28,20},{1,9},{5,13},{25,17},{29,21},{2,10},{... | collective-permute-start | bytes 1411208 | tf_op jit(solution)/shard_map/ppermute | solution.py:100
  386.9 9.0 %collective-permute-start.36 = (bf16[70,1120]{1,0:T(8,128)(2,1)S(1)}, bf16[70,1120]{1,0:T(8,128)(2,1)S(1)}, u32[]{:S(2)}, u32[]{:S(2)}) collective-permute-start(bf16[70,1120]{1,0:T(8,128)(2,1)S(1)} %add_convert_fusion.31), channel_id=1, source_target_pairs={{8,0},{12,4},{16,24},{20,28},{9,1},{13,5},{17,25},{21,29},{10,2},{... | collective-permute-start | bytes 470408 | tf_op jit(solution)/shard_map/ppermute | solution.py:100
  388.4 74.3 %collective-permute-start.55 = (bf16[560,1120]{1,0:T(8,128)(2,1)S(1)}, bf16[560,1120]{1,0:T(8,128)(2,1)S(1)}, u32[]{:S(2)}, u32[]{:S(2)}) collective-permute-start(bf16[560,1120]{1,0:T(8,128)(2,1)S(1)} %pad_maximum_fusion.4), channel_id=1, source_target_pairs={{8,0},{12,4},{16,24},{20,28},{9,1},{13,5},{17,25},{21,29},{10,2},{... | collective-permute-start | bytes 3763208 | tf_op jit(solution)/shard_map/ppermute | solution.py:100
  402.0 63.7 %collective-permute-start.65 = (bf16[560,1120]{1,0:T(8,128)(2,1)S(1)}, bf16[560,1120]{1,0:T(8,128)(2,1)S(1)}, u32[]{:S(2)}, u32[]{:S(2)}) collective-permute-start(bf16[560,1120]{1,0:T(8,128)(2,1)S(1)} %pad_maximum_fusion.5), channel_id=1, source_target_pairs={{8,0},{12,4},{16,24},{20,28},{9,1},{13,5},{17,25},{21,29},{10,2},{... | collective-permute-start | bytes 3763208 | tf_op jit(solution)/shard_map/ppermute | solution.py:100
  403.4 53.9 %collective-permute-start.42 = (bf16[140,1120]{1,0:T(8,128)(2,1)S(1)}, bf16[140,1120]{1,0:T(8,128)(2,1)S(1)}, u32[]{:S(2)}, u32[]{:S(2)}) collective-permute-start(bf16[140,1120]{1,0:T(8,128)(2,1)S(1)} %pad_maximum_fusion.12), channel_id=1, source_target_pairs={{8,0},{12,4},{16,24},{20,28},{9,1},{13,5},{17,25},{21,29},{10,2},{... | collective-permute-start | bytes 940808 | tf_op jit(solution)/shard_map/ppermute | solution.py:100
  411.6 50.0 %collective-permute-start.15 = (bf16[384,1120]{0,1:T(8,128)(2,1)S(1)}, bf16[384,1120]{0,1:T(8,128)(2,1)S(1)}, u32[]{:S(2)}, u32[]{:S(2)}) collective-permute-start(bf16[384,1120]{0,1:T(8,128)(2,1)S(1)} %add_convert_fusion.5), channel_id=1, source_target_pairs={{0,2},{1,3},{2,0},{3,1},{4,6},{5,7},{6,4},{7,5},{8,10},{9,11},{10,... | collective-permute-start | bytes 2580488 | tf_op jit(solution)/shard_map/ppermute | solution.py:30
  413.2 46.1 %collective-permute-start.22 = (bf16[280,840]{1,0:T(8,128)(2,1)S(1)}, bf16[280,840]{1,0:T(8,128)(2,1)S(1)}, u32[]{:S(2)}, u32[]{:S(2)}) collective-permute-start(bf16[280,840]{1,0:T(8,128)(2,1)S(1)} %add_convert_fusion.23), channel_id=1, source_target_pairs={{8,16},{12,20},{16,8},{20,12},{9,17},{13,21},{17,9},{21,13},{10,18... | collective-permute-start | bytes 1411208 | tf_op jit(solution)/shard_map/ppermute | solution.py:100
  459.4 14.3 %collective-permute-start.23 = (bf16[280,840]{1,0:T(8,128)(2,1)S(1)}, bf16[280,840]{1,0:T(8,128)(2,1)S(1)}, u32[]{:S(2)}, u32[]{:S(2)}) collective-permute-start(bf16[280,840]{1,0:T(8,128)(2,1)S(1)} %add_convert_fusion.22), channel_id=1, source_target_pairs={{8,0},{12,4},{16,24},{20,28},{9,1},{13,5},{17,25},{21,29},{10,2},{... | collective-permute-start | bytes 1411208 | tf_op jit(solution)/shard_map/ppermute | solution.py:100
  460.9 13.5 %collective-permute-start.27 = (bf16[280,840]{1,0:T(8,128)(2,1)S(1)}, bf16[280,840]{1,0:T(8,128)(2,1)S(1)}, u32[]{:S(2)}, u32[]{:S(2)}) collective-permute-start(bf16[280,840]{1,0:T(8,128)(2,1)S(1)} %add_convert_fusion.21), channel_id=1, source_target_pairs={{8,12},{12,8},{16,20},{20,16},{9,13},{13,9},{17,21},{21,17},{10,14... | collective-permute-start | bytes 1411208 | tf_op jit(solution)/shard_map/ppermute | solution.py:100
  462.7 31.2 %collective-permute-start.16 = (bf16[384,1120]{0,1:T(8,128)(2,1)}, bf16[384,1120]{0,1:T(8,128)(2,1)}, u32[]{:S(2)}, u32[]{:S(2)}) collective-permute-start(bf16[384,1120]{0,1:T(8,128)(2,1)} %add_convert_fusion.4), channel_id=1, source_target_pairs={{0,1},{1,0},{2,3},{3,2},{4,5},{5,4},{6,7},{7,6},{8,9},{9,8},{10,11... | collective-permute-start | bytes 2580488 | tf_op jit(solution)/shard_map/ppermute | solution.py:26
  473.8 11.6 %collective-permute-start.24 = (bf16[280,840]{1,0:T(8,128)(2,1)S(1)}, bf16[280,840]{1,0:T(8,128)(2,1)S(1)}, u32[]{:S(2)}, u32[]{:S(2)}) collective-permute-start(bf16[280,840]{1,0:T(8,128)(2,1)S(1)} %broadcast_select_fusion.25), channel_id=1, source_target_pairs={{0,4},{4,0},{8,12},{12,8},{16,20},{20,16},{24,28},{28,24},{1,5},{5... | collective-permute-start | bytes 1411208 | tf_op jit(solution)/shard_map/ppermute | solution.py:100
  475.3 15.5 %collective-permute-start.28 = (bf16[280,840]{1,0:T(8,128)(2,1)}, bf16[280,840]{1,0:T(8,128)(2,1)}, u32[]{:S(2)}, u32[]{:S(2)}) collective-permute-start(bf16[280,840]{1,0:T(8,128)(2,1)} %add_convert_fusion.20), channel_id=1, source_target_pairs={{8,16},{12,20},{16,8},{20,12},{9,17},{13,21},{17,9},{21,13},{10,18... | collective-permute-start | bytes 1411208 | tf_op jit(solution)/shard_map/ppermute | solution.py:100
  492.3 32.1 %collective-permute-start.29 = (bf16[560,840]{1,0:T(8,128)(2,1)S(1)}, bf16[560,840]{1,0:T(8,128)(2,1)S(1)}, u32[]{:S(2)}, u32[]{:S(2)}) collective-permute-start(bf16[560,840]{1,0:T(8,128)(2,1)S(1)} %pad_maximum_fusion.6), channel_id=1, source_target_pairs={{8,0},{12,4},{16,24},{20,28},{9,1},{13,5},{17,25},{21,29},{10,2},{... | collective-permute-start | bytes 2822408 | tf_op jit(solution)/shard_map/ppermute | solution.py:100
  500.8 12.1 %collective-permute-start.18 = (f32[2,1120]{1,0:T(2,128)S(1)}, f32[2,1120]{1,0:T(2,128)S(1)}, u32[]{:S(2)}, u32[]{:S(2)}) collective-permute-start(f32[2,1120]{1,0:T(2,128)S(1)} %fusion.94), channel_id=1, source_target_pairs={{0,16},{4,20},{8,24},{12,28},{16,0},{20,4},{24,8},{28,12},{1,17},{... | collective-permute-start | bytes 26888 | tf_op jit(solution)/shard_map/ppermute | solution.py:100
  512.9 10.9 %collective-permute-start.19 = (f32[2,1120]{1,0:T(2,128)S(1)}, f32[2,1120]{1,0:T(2,128)S(1)}, u32[]{:S(2)}, u32[]{:S(2)}) collective-permute-start(f32[2,1120]{1,0:T(2,128)S(1)} %fusion.134), channel_id=1, source_target_pairs={{0,8},{4,12},{8,0},{12,4},{16,24},{20,28},{24,16},{28,20},{1,9},{5... | collective-permute-start | bytes 26888 | tf_op jit(solution)/shard_map/ppermute | solution.py:100
  (55 other events, 530.4 us)
